TPU v7x, 128 devices: a whole 4x4x4 slice. The times are simulated.
128 devices in a mesh: outer: 8 (over y, core), inner: 16 (over z, x).
Axes of the slice: x: 4, y: 4, z: 4, core: 2. Of those that a mesh axis runs over, the one named last changes fastest.
Arguments:
- layer_input: bfloat16 [16384, 7168], P(('outer', 'inner')), may hold values from -6 to 6
- out_grad: bfloat16 [16384, 7168], P(('outer', 'inner')), may hold values from -3 to 3
- expert_ids: int32 [16384, 8], P(('outer', 'inner')), may hold values from 0 to 255, as said below
- route_scales: float32 [16384, 8], P(('outer', 'inner')), may hold values from 0.25 to 2.5
- w_gate: bfloat16 [8, 7168, 2048], P('outer', None, 'inner'), may hold values from -0.0625 to 0.0625
- w_up: bfloat16 [8, 7168, 2048], P('outer', None, 'inner'), may hold values from -0.0625 to 0.0625
- w_down: bfloat16 [8, 2048, 7168], P('outer', 'inner'), may hold values from -0.125 to 0.125
Outputs:
- in_grad: bfloat16 [16384, 7168], P(('outer', 'inner'))
- grad_w_gate: float32 [8, 7168, 2048], P('outer', None, 'inner')
- grad_w_up: float32 [8, 7168, 2048], P('outer', None, 'inner')
- grad_w_down: float32 [8, 2048, 7168], P('outer', 'inner')
Inputs may be any that keep to these rules, and one draw needn't show every extreme that they name: `expert_ids`: each row names 8 different experts. In each device's aligned block of 128 rows at most 6 rows name any one expert below 8, and in every draw one expert below 8 is named by exactly 6 rows of every block.
All inputs are finite; a program needn't handle non-finite values.
Results may differ from a plain program's by a relative error of at most 0.014.
Values may be sent and summed in bfloat16 or wider, within the bound.
A program may use at most 192 MiB of HBM per device.

v0:
```python
import jax
import jax.numpy as jnp
from jax import lax
from jax.sharding import PartitionSpec as P

CAP = 6


def shards(layer_input, out_grad, expert_ids, route_scales, w_gate, w_up, w_down):
    tok_count = layer_input.shape[0]
    model_width = layer_input.shape[1]
    n_outer = lax.axis_size("outer")
    top_count = expert_ids.shape[1]
    slot_count = n_outer * CAP
    route_ids = expert_ids.reshape(-1)
    onehot = (route_ids[:, None] == jnp.arange(n_outer, dtype=jnp.int32)[None, :]).astype(jnp.int32)
    position = jnp.sum((jnp.cumsum(onehot, axis=0) - onehot) * onehot, axis=1)
    slot = jnp.where(route_ids < n_outer, route_ids * CAP + position, -1)
    picks = slot[:, None] == jnp.arange(slot_count, dtype=jnp.int32)[None, :]
    place = jnp.any(picks.reshape(tok_count, top_count, slot_count), axis=1).astype(jnp.bfloat16)
    slot_scale = jnp.sum(jnp.where(picks, route_scales.reshape(-1)[:, None], 0.0), axis=0)
    take_rows = (((0,), (0,)), ((), ()))
    send_x = lax.dot_general(
        place, layer_input, take_rows, preferred_element_type=jnp.float32
    ).astype(jnp.bfloat16)
    send_dy = lax.dot_general(place, out_grad, take_rows, preferred_element_type=jnp.float32)
    routed = (send_dy * slot_scale[:, None]).astype(jnp.bfloat16)
    send_x = send_x.reshape(n_outer, CAP, model_width)
    routed = routed.reshape(n_outer, CAP, model_width)
    gate_w = w_gate[0]
    up_w = w_up[0]
    down_w = w_down[0]
    got_x, got_gy = (
        lax.all_to_all(send_x, "outer", split_axis=0, concat_axis=0, tiled=True),
        lax.all_to_all(routed, "outer", split_axis=0, concat_axis=0, tiled=True),
    )
    rows_x = lax.all_gather(got_x.reshape(-1, model_width), "inner", axis=0, tiled=True)
    rows_gy = lax.all_gather(got_gy.reshape(-1, model_width), "inner", axis=0, tiled=True)
    gate = jnp.dot(rows_x, gate_w, preferred_element_type=jnp.float32)
    up_val = jnp.dot(rows_x, up_w, preferred_element_type=jnp.float32)
    sigmoid_gate = jax.nn.sigmoid(gate)
    silu_gate = gate * sigmoid_gate
    act = (silu_gate * up_val).astype(jnp.bfloat16)
    hid_grad = lax.dot_general(
        rows_gy, down_w, (((1,), (1,)), ((), ())), preferred_element_type=jnp.float32
    )
    gate_grad = (hid_grad * up_val * sigmoid_gate * (1.0 + gate * (1.0 - sigmoid_gate))).astype(
        jnp.bfloat16
    )
    up_grad = (hid_grad * silu_gate).astype(jnp.bfloat16)
    gate_sum = lax.dot_general(rows_x, gate_grad, take_rows, preferred_element_type=jnp.float32)
    up_sum = lax.dot_general(rows_x, up_grad, take_rows, preferred_element_type=jnp.float32)
    down_sum = lax.dot_general(act, rows_gy, take_rows, preferred_element_type=jnp.float32)
    gate_store = gate_grad
    up_store = up_grad
    carry = (gate_sum, up_sum, down_sum, gate_store, up_store)
    grad_gate, grad_up, grad_down, gate_store, up_store = carry
    term = lax.dot_general(
        gate_store, gate_w, (((1,), (1,)), ((), ())), preferred_element_type=jnp.float32
    )
    mine = lax.psum_scatter(
        (
            term
            + lax.dot_general(
                up_store, up_w, (((1,), (1,)), ((), ())), preferred_element_type=jnp.float32
            )
        ).astype(jnp.bfloat16),
        "inner",
        scatter_dimension=0,
        tiled=True,
    ).astype(jnp.float32)
    mine = mine.astype(jnp.bfloat16).reshape(n_outer, CAP, model_width)
    back = lax.all_to_all(mine, "outer", split_axis=0, concat_axis=0, tiled=True).reshape(
        slot_count, model_width
    )
    in_grad = jnp.dot(place, back, preferred_element_type=jnp.float32).astype(jnp.bfloat16)
    return (in_grad, grad_gate[None], grad_up[None], grad_down[None])


def solution(mesh):
    return jax.shard_map(
        shards,
        mesh=mesh,
        in_specs=(
            P(("outer", "inner"), None),
            P(("outer", "inner"), None),
            P(("outer", "inner"), None),
            P(("outer", "inner"), None),
            P("outer", None, "inner"),
            P("outer", None, "inner"),
            P("outer", "inner", None),
        ),
        out_specs=(
            P(("outer", "inner"), None),
            P("outer", None, "inner"),
            P("outer", None, "inner"),
            P("outer", "inner", None),
        ),
        check_vma=False,
    )
```

profile of v0, /device:TPU:1, one launch (start us, length us, event | category | flops | bytes accessed | tf_op | source)
XLA Modules:
  0.0 355.3 jit_solution(1478537319193128124)
XLA Ops:
  7.2 0.9 copy.27
  8.3 2.3 reduce-window.6
  11.3 0.7 add_select_fusion.1
  12.1 1.9 convolution_convert_fusion.1
  14.2 19.7 %all_to_all.15 = bf16[8,6,7168]{2,1,0:T(8,128)(2,1)} all-to-all(bf16[8,6,7168]{2,1,0:T(8,128)(2,1)S(1)} %reshape.72), channel_id=1, replica_groups=mesh['outer'=8,'inner'=16] {'outer'}, dimensions={0} | all-to-all | bytes 1376256 | tf_op jit(solution)/shard_map/all_to_all | solution.py:34
  33.9 2.3 reshape.73
  36.6 1.9 fusion
  38.7 17.8 %all_to_all.16 = bf16[8,6,7168]{2,1,0:T(8,128)(2,1)} all-to-all(bf16[8,6,7168]{2,1,0:T(8,128)(2,1)S(1)} %reshape.70), channel_id=1, replica_groups=mesh['outer'=8,'inner'=16] {'outer'}, dimensions={0} | all-to-all | bytes 1376256 | tf_op jit(solution)/shard_map/all_to_all | solution.py:35
  56.5 2.3 reshape.71
  58.8 61.0 %all-gather.5.cloned.1.call-done = bf16[768,7168]{1,0:T(8,128)(2,1)} async-done(((bf16[48,7168]{1,0:T(8,128)(2,1)}), bf16[768,7168]{1,0:T(8,128)(2,1)}) %all-gather.5.cloned.1.call-update) | async-done | bytes 11010064 | tf_op jit(solution)/shard_map/all_gather | solution.py:37
  119.8 7.2 %fusion.3 = f32[768,128]{1,0:T(8,128)S(1)} fusion(bf16[768,7168]{1,0:T(8,128)(2,1)} %all-gather.5.cloned.1.call-done, bf16[1,7168,128]{2,1,0:T(8,128)(2,1)S(1)} %copy-done), kind=kOutput, calls=%fused_computation.10 | convolution fusion | flops 1409286144 | bytes 13238272 | tf_op jit(solution)/shard_map/dot_general | solution.py:39
  127.6 3.0 fusion.6
  130.6 74.4 %all-gather.3.cloned.1.call-done = bf16[768,7168]{1,0:T(8,128)(2,1)} async-done(((bf16[48,7168]{1,0:T(8,128)(2,1)}), bf16[768,7168]{1,0:T(8,128)(2,1)}) %all-gather.3.cloned.1.call-update) | async-done | bytes 11010064 | tf_op jit(solution)/shard_map/all_gather | solution.py:38
  205.0 7.6 %multiply_convert_fusion.1 = (bf16[768,128]{1,0:T(8,128)(2,1)S(1)}, bf16[768,128]{1,0:T(8,128)(2,1)S(1)}) fusion(f32[768,128]{1,0:T(8,128)S(1)} %fusion.3, f32[768,128]{1,0:T(8,128)S(1)} %fusion.6, bf16[768,7168]{1,0:T(8,128)(2,1)} %all-gather.3.cloned.1.call-done, bf16[1,128,7168]{2,1,0:T(8,128)(2,1)} %param.13), kind=kOutput, calls=%fused_computation.18 | convolution fusion | flops 1410564096 | bytes 14024704 | tf_op jit(solution)/shard_map/dot_general | solution.py:44
  212.7 9.0 %fusion.1 = f32[768,7168]{1,0:T(8,128)} fusion(bf16[768,128]{1,0:T(8,128)(2,1)S(1)} %get-tuple-element.5, bf16[1,7168,128]{2,1,0:T(8,128)(2,1)S(1)} %copy-done), kind=kOutput, calls=%fused_computation.8 | convolution fusion | flops 1409286144 | bytes 24051712 | tf_op jit(solution)/shard_map/dot_general | solution.py:58
  221.7 13.2 %add_convert_fusion = bf16[768,7168]{1,0:T(8,128)(2,1)} fusion(f32[768,7168]{1,0:T(8,128)} %fusion.1, bf16[768,128]{1,0:T(8,128)(2,1)S(1)} %get-tuple-element.4, bf16[1,7168,128]{2,1,0:T(8,128)(2,1)} %param.12), kind=kOutput, calls=%fused_computation | convolution fusion | flops 1420296192 | bytes 35061760 | tf_op jit(solution)/shard_map/dot_general | solution.py:64
  234.9 9.0 %convolution_bitcast_fusion.1 = f32[1,7168,128]{2,1,0:T(8,128)} fusion(bf16[768,7168]{1,0:T(8,128)(2,1)} %all-gather.5.cloned.1.call-done, bf16[768,128]{1,0:T(8,128)(2,1)S(1)} %get-tuple-element.4), kind=kOutput, calls=%fused_computation.2 | convolution fusion | flops 1409286144 | bytes 14876672 | tf_op jit(solution)/shard_map/dot_general | solution.py:52
  243.9 9.2 %convolution_bitcast_fusion.2 = f32[1,7168,128]{2,1,0:T(8,128)} fusion(bf16[768,7168]{1,0:T(8,128)(2,1)} %all-gather.5.cloned.1.call-done, bf16[768,128]{1,0:T(8,128)(2,1)S(1)} %get-tuple-element.5), kind=kOutput, calls=%fused_computation.3 | convolution fusion | flops 1409286144 | bytes 14876672 | tf_op jit(solution)/shard_map/dot_general | solution.py:51
  253.1 72.1 %reduce-scatter.2.cloned.1.call-done = bf16[48,7168]{1,0:T(8,128)(2,1)} async-done(((bf16[768,7168]{1,0:T(8,128)(2,1)}), bf16[48,7168]{1,0:T(8,128)(2,1)}) %reduce-scatter.2.cloned.1.call-update) | async-done | bytes 688144 | tf_op jit(solution)/shard_map/reduce_scatter | solution.py:61
  325.1 2.3 reshape.74
  327.4 5.5 %all-to-all-start.2 = ((bf16[8,6,7168]{2,1,0:T(8,128)(2,1)}), bf16[8,6,7168]{2,1,0:T(8,128)(2,1)S(1)}, u32[]{:S(2)}, u32[]{:S(2)}) async-start(bf16[8,6,7168]{2,1,0:T(8,128)(2,1)} %reshape.74), calls=%async_computation.3 | async-start | bytes 1835008 | tf_op jit(solution)/shard_map/all_to_all | solution.py:73
  332.9 7.8 %convolution_bitcast_fusion = f32[1,128,7168]{2,1,0:T(8,128)} fusion(bf16[768,7168]{1,0:T(8,128)(2,1)} %all-gather.3.cloned.1.call-done, f32[768,128]{1,0:T(8,128)S(1)} %fusion.6, f32[768,128]{1,0:T(8,128)S(1)} %fusion.3), kind=kOutput, calls=%fused_computation.1 | convolution fusion | flops 1409875968 | bytes 15466496 | tf_op jit(solution)/shard_map/dot_general | solution.py:53
  340.7 5.9 %all-to-all-done.2 = bf16[8,6,7168]{2,1,0:T(8,128)(2,1)S(1)} async-done(((bf16[8,6,7168]{2,1,0:T(8,128)(2,1)}), bf16[8,6,7168]{2,1,0:T(8,128)(2,1)S(1)}, u32[]{:S(2)}, u32[]{:S(2)}) %all-to-all-start.2) | async-done | bytes 688160 | tf_op jit(solution)/shard_map/all_to_all | solution.py:73
  346.8 1.9 convolution_convert_fusion
  (33 shorter events, 2.8 us)
Async XLA Ops:
  7.2 112.6 %copy-start = (bf16[1,7168,128]{2,1,0:T(8,128)(2,1)S(1)}, bf16[1,7168,128]{2,1,0:T(8,128)(2,1)}, u32[]{:S(2)}) copy-start(bf16[1,7168,128]{2,1,0:T(8,128)(2,1)} %param.11) | copy-start | bytes 5505028
  7.2 112.6 %all-gather.5.cloned.1.call-start = ((), (), s32[]{:S(2)}) async-start(), calls=%async_computation.5 | async-start | bytes 11698176 | tf_op jit(solution)/shard_map/all_gather | solution.py:37
  12.0 24.2 %copy-start.4 = (f32[128,8]{0,1:T(8,128)S(1)}, f32[128,8]{0,1:T(8,128)}, u32[]{:S(2)}) copy-start(f32[128,8]{0,1:T(8,128)} %param.10) | copy-start | bytes 12292
  36.2 168.8 %all-gather.3.cloned.1.call-start = ((), (), s32[]{:S(2)}) async-start(), calls=%async_computation.4 | async-start | bytes 11698176 | tf_op jit(solution)/shard_map/all_gather | solution.py:38
  58.8 266.4 %reduce-scatter.2.cloned.1.call-start = ((), (), s32[]{:S(2)}) async-start(), calls=%async_computation.6 | async-start | bytes 11698176 | tf_op jit(solution)/shard_map/reduce_scatter | solution.py:61
  119.8 7.3 %copy-start.2 = (bf16[768,7168]{1,0:T(8,128)(2,1)S(1)}, bf16[768,7168]{1,0:T(8,128)(2,1)}, u32[]{:S(2)}) copy-start(bf16[768,7168]{1,0:T(8,128)(2,1)} %all-gather.5.cloned.1.call-done) | copy-start | bytes 33030148
  119.8 7.8 %copy-start.3 = (bf16[1,7168,128]{2,1,0:T(8,128)(2,1)S(1)}, bf16[1,7168,128]{2,1,0:T(8,128)(2,1)}, u32[]{:S(2)}) copy-start(bf16[1,7168,128]{2,1,0:T(8,128)(2,1)} %param.12) | copy-start | bytes 5505028
  327.4 19.2 %all-to-all-start.2 = ((bf16[8,6,7168]{2,1,0:T(8,128)(2,1)}), bf16[8,6,7168]{2,1,0:T(8,128)(2,1)S(1)}, u32[]{:S(2)}, u32[]{:S(2)}) async-start(bf16[8,6,7168]{2,1,0:T(8,128)(2,1)} %reshape.74), calls=%async_computation.3 | async-start | bytes 1835008 | tf_op jit(solution)/shard_map/all_to_all | solution.py:73
  332.9 15.9 %copy-start.1 = (bf16[1,7168,128]{2,1,0:T(8,128)(2,1)S(1)}, bf16[1,7168,128]{2,1,0:T(8,128)(2,1)}, u32[]{:S(2)}) copy-start(bf16[1,7168,128]{2,1,0:T(8,128)(2,1)} %param.11) | copy-start | bytes 5505028
Sparse Core Ops, SparseCore 0:
  36.3 83.4 all-gather.4
  122.5 82.4 all-gather.2
  235.0 90.0 reduce-scatter.1
where the time goes:
time: 356 us; the launch traced here: 355 us
  waiting for transfers between devices  213 us (60%)
  matrix products  71.7 us (20%)
  blocking collectives  37.4 us (11%)
  between operations  13.9 us (4%)
  local copies, waits for them, and re-layouts  9.88 us (3%)
  starting transfers between devices  5.58 us (2%)
    all_gather x1, waiting for transfers between devices, shards(): lax.all_gather(got_gy.reshape(-1, model_width), 'inner', axis=0, tiled=True)  74.4 us
    reduce_scatter x1, waiting for transfers between devices, shards(): lax.psum_scatter((term + lax.dot_general(up_store, up_w, (((1,), (1,)), (...  72.1 us
    all_gather x1, waiting for transfers between devices, shards(): lax.all_gather(got_x.reshape(-1, model_width), 'inner', axis=0, tiled=True)  61 us
    all_to_all x1, blocking collectives, shards(): lax.all_to_all(send_x, 'outer', split_axis=0, concat_axis=0, tiled=True)  19.7 us
    all_to_all x1, blocking collectives, shards(): lax.all_to_all(routed, 'outer', split_axis=0, concat_axis=0, tiled=True)  17.8 us
    dot_general x1, matrix products, shards(): lax.dot_general(up_store, up_w, (((1,), (1,)), ((), ())), preferred_eleme...  13.2 us
    dot_general x1, matrix products, shards(): lax.dot_general(rows_x, gate_grad, take_rows, preferred_element_type=jnp....  9.15 us
    dot_general x1, matrix products, shards(): lax.dot_general(rows_x, up_grad, take_rows, preferred_element_type=jnp.fl...  9.03 us
  transfers between devices with their start and end apart: 4, of which 4 were waited for; matrix products, arithmetic and copies ran while one was open for 12% of the time, Pallas kernels for 0%

commit v1 on v0

--- a/solution.py
+++ b/solution.py
@@ -34,7 +34,12 @@
         lax.all_to_all(send_x, "outer", split_axis=0, concat_axis=0, tiled=True),
         lax.all_to_all(routed, "outer", split_axis=0, concat_axis=0, tiled=True),
     )
-    rows_x = lax.all_gather(got_x.reshape(-1, model_width), "inner", axis=0, tiled=True)
+    rows_x = jnp.concatenate(
+        lax.all_to_all(
+            jnp.stack([got_x.reshape(-1, model_width)] * lax.axis_size("inner")), "inner", 0, 0
+        ),
+        axis=0,
+    )
     rows_gy = lax.all_gather(got_gy.reshape(-1, model_width), "inner", axis=0, tiled=True)
     gate = jnp.dot(rows_x, gate_w, preferred_element_type=jnp.float32)
     up_val = jnp.dot(rows_x, up_w, preferred_element_type=jnp.float32)

time: 356 us -> 395 us (1.11)
  blocking collectives: 37.4 us -> 213 us
  waiting for transfers between devices: 213 us -> 74.2 us
  local copies, waits for them, and re-layouts: 9.88 us -> 16 us
  matrix products: 71.7 us -> 67.6 us
    all_to_all x0 -> x1, blocking collectives: none -> 176 us  [shards(): lax.all_to_all(jnp.stack([got_x.reshape(-1, model_width)] * lax.axis_size...]
    all_gather x1, waiting for transfers between devices: 74.4 us -> 0.02 us  [shards(): lax.all_gather(got_gy.reshape(-1, model_width), 'inner', axis=0, tiled=True)]
    all_gather x1 -> x0, waiting for transfers between devices: 61 us -> none  [shards(): lax.all_gather(got_x.reshape(-1, model_width), 'inner', axis=0, tiled=True)]
    another operation x0 -> x2, local copies, waits for them, and re-layouts: none -> 6.97 us  [shards(): jnp.stack([got_x.reshape(-1, model_width)] * lax.axis_size('inner'))]
    dot_general x1, matrix products: 7.22 us -> 2.99 us  [shards(): gate = jnp.dot(rows_x, gate_w, preferred_element_type=jnp.float32)]
  transfers between devices with their start and end apart: 4 -> 3, of which waited for: 4 -> 2; matrix products, arithmetic and copies ran while one was open for 12% -> 10% of each run, Pallas kernels for 0% -> 0%
where the time goes in v1:
time: 395 us; the launch traced here: 394 us
  blocking collectives  213 us (54%)
  waiting for transfers between devices  74.2 us (19%)
  matrix products  67.6 us (17%)
  local copies, waits for them, and re-layouts  16 us (4%)
  between operations  14.2 us (4%)
  starting transfers between devices  5.63 us (1%)
    all_to_all x1, blocking collectives, shards(): lax.all_to_all(jnp.stack([got_x.reshape(-1, model_width)] * lax.axis_size...  176 us
    reduce_scatter x1, waiting for transfers between devices, shards(): lax.psum_scatter((term + lax.dot_general(up_store, up_w, (((1,), (1,)), (...  68.3 us
    all_to_all x1, blocking collectives, shards(): lax.all_to_all(routed, 'outer', split_axis=0, concat_axis=0, tiled=True)  19.7 us
    all_to_all x1, blocking collectives, shards(): lax.all_to_all(send_x, 'outer', split_axis=0, concat_axis=0, tiled=True)  17.8 us
    dot_general x1, matrix products, shards(): lax.dot_general(up_store, up_w, (((1,), (1,)), ((), ())), preferred_eleme...  13.2 us
    dot_general x1, matrix products, shards(): lax.dot_general(rows_x, gate_grad, take_rows, preferred_element_type=jnp....  9.19 us
    dot_general x1, matrix products, shards(): lax.dot_general(rows_x, up_grad, take_rows, preferred_element_type=jnp.fl...  9.03 us
    dot_general x1, matrix products, shards(): lax.dot_general(gate_store, gate_w, (((1,), (1,)), ((), ())), preferred_e...  9.02 us
  transfers between devices with their start and end apart: 3, of which 2 were waited for; matrix products, arithmetic and copies ran while one was open for 10% of the time, Pallas kernels for 0%

profile of v1, /device:TPU:1, one launch (start us, length us, event | category | flops | bytes accessed | tf_op | source)
XLA Modules:
  0.0 394.0 jit_solution(2562316342508416544)
XLA Ops:
  7.2 0.9 copy.27
  8.3 2.3 reduce-window.6
  13.1 1.9 fusion
  15.2 19.7 %all_to_all.20 = bf16[8,6,7168]{2,1,0:T(8,128)(2,1)} all-to-all(bf16[8,6,7168]{2,1,0:T(8,128)(2,1)S(1)} %reshape.72), channel_id=1, replica_groups=mesh['outer'=8,'inner'=16] {'outer'}, dimensions={0} | all-to-all | bytes 1376256 | tf_op jit(solution)/shard_map/all_to_all | solution.py:35
  34.9 2.3 reshape.73
  37.2 1.9 convolution_convert_fusion.1
  39.4 17.8 %all_to_all.21 = bf16[8,6,7168]{2,1,0:T(8,128)(2,1)} all-to-all(bf16[8,6,7168]{2,1,0:T(8,128)(2,1)S(1)} %reshape.74), channel_id=1, replica_groups=mesh['outer'=8,'inner'=16] {'outer'}, dimensions={0} | all-to-all | bytes 1376256 | tf_op jit(solution)/shard_map/all_to_all | solution.py:34
  57.1 1.4 stack_reshape.2
  58.6 5.5 %stack.3 = bf16[16,48,7168]{2,1,0:T(8,128)(2,1)} broadcast(bf16[48,7168]{1,0:T(8,128)(2,1)S(1)} %stack_reshape.2), dimensions={1,2} | broadcast | bytes 11698176 | tf_op jit(solution)/shard_map/stack | solution.py:39
  64.1 175.7 %all_to_all.22 = bf16[16,48,7168]{2,1,0:T(8,128)(2,1)S(1)} all-to-all(bf16[16,48,7168]{2,1,0:T(8,128)(2,1)} %stack.3), channel_id=1, replica_groups=mesh['outer'=8,'inner'=16] {'inner'}, dimensions={0} | all-to-all | bytes 22020096 | tf_op jit(solution)/shard_map/all_to_all | solution.py:38
  239.8 3.0 fusion.3
  242.8 1.3 copy-done.2
  244.1 3.0 fusion.6
  247.1 7.6 %multiply_convert_fusion.1 = (bf16[768,128]{1,0:T(8,128)(2,1)S(1)}, bf16[768,128]{1,0:T(8,128)(2,1)S(1)}) fusion(f32[768,128]{1,0:T(8,128)S(1)} %fusion.3, f32[768,128]{1,0:T(8,128)S(1)} %fusion.6, bf16[768,7168]{1,0:T(8,128)(2,1)} %all-gather.2.cloned.1.call-done, bf16[1,128,7168]{2,1,0:T(8,128)(2,1)} %param.13), kind=kOutput, calls=%fused_computation.18 | convolution fusion | flops 1410564096 | bytes 14024704 | tf_op jit(solution)/shard_map/dot_general | solution.py:49
  254.8 9.0 %fusion.1 = f32[768,7168]{1,0:T(8,128)} fusion(bf16[768,128]{1,0:T(8,128)(2,1)S(1)} %get-tuple-element.5, bf16[1,7168,128]{2,1,0:T(8,128)(2,1)S(1)} %copy-done), kind=kOutput, calls=%fused_computation.8 | convolution fusion | flops 1409286144 | bytes 24051712 | tf_op jit(solution)/shard_map/dot_general | solution.py:63
  263.8 13.2 %add_convert_fusion = bf16[768,7168]{1,0:T(8,128)(2,1)} fusion(f32[768,7168]{1,0:T(8,128)} %fusion.1, bf16[768,128]{1,0:T(8,128)(2,1)S(1)} %get-tuple-element.4, bf16[1,7168,128]{2,1,0:T(8,128)(2,1)} %param.12), kind=kOutput, calls=%fused_computation | convolution fusion | flops 1420296192 | bytes 35061760 | tf_op jit(solution)/shard_map/dot_general | solution.py:69
  277.0 9.0 %convolution_bitcast_fusion.1 = f32[1,7168,128]{2,1,0:T(8,128)} fusion(bf16[768,7168]{1,0:T(8,128)(2,1)} %bitcast.59, bf16[768,128]{1,0:T(8,128)(2,1)S(1)} %get-tuple-element.4), kind=kOutput, calls=%fused_computation.2 | convolution fusion | flops 1409286144 | bytes 14876672 | tf_op jit(solution)/shard_map/dot_general | solution.py:57
  286.0 9.2 %convolution_bitcast_fusion.2 = f32[1,7168,128]{2,1,0:T(8,128)} fusion(bf16[768,7168]{1,0:T(8,128)(2,1)} %bitcast.60, bf16[768,128]{1,0:T(8,128)(2,1)S(1)} %get-tuple-element.5), kind=kOutput, calls=%fused_computation.3 | convolution fusion | flops 1409286144 | bytes 14876672 | tf_op jit(solution)/shard_map/dot_general | solution.py:56
  295.2 68.3 %reduce-scatter.2.cloned.1.call-done = bf16[48,7168]{1,0:T(8,128)(2,1)} async-done(((bf16[768,7168]{1,0:T(8,128)(2,1)}), bf16[48,7168]{1,0:T(8,128)(2,1)}) %reduce-scatter.2.cloned.1.call-update) | async-done | bytes 688144 | tf_op jit(solution)/shard_map/reduce_scatter | solution.py:66
  363.5 2.3 reshape.76
  365.8 5.6 %all-to-all-start.3 = ((bf16[8,6,7168]{2,1,0:T(8,128)(2,1)}), bf16[8,6,7168]{2,1,0:T(8,128)(2,1)S(1)}, u32[]{:S(2)}, u32[]{:S(2)}) async-start(bf16[8,6,7168]{2,1,0:T(8,128)(2,1)} %reshape.76), calls=%async_computation.4 | async-start | bytes 1835008 | tf_op jit(solution)/shard_map/all_to_all | solution.py:78
  371.3 7.8 %convolution_bitcast_fusion = f32[1,128,7168]{2,1,0:T(8,128)} fusion(bf16[768,7168]{1,0:T(8,128)(2,1)} %all-gather.2.cloned.1.call-done, f32[768,128]{1,0:T(8,128)S(1)} %fusion.6, f32[768,128]{1,0:T(8,128)S(1)} %fusion.3), kind=kOutput, calls=%fused_computation.1 | convolution fusion | flops 1409875968 | bytes 15466496 | tf_op jit(solution)/shard_map/dot_general | solution.py:58
  379.1 5.9 %all-to-all-done.3 = bf16[8,6,7168]{2,1,0:T(8,128)(2,1)S(1)} async-done(((bf16[8,6,7168]{2,1,0:T(8,128)(2,1)}), bf16[8,6,7168]{2,1,0:T(8,128)(2,1)S(1)}, u32[]{:S(2)}, u32[]{:S(2)}) %all-to-all-start.3) | async-done | bytes 688160 | tf_op jit(solution)/shard_map/all_to_all | solution.py:78
  385.3 1.9 convolution_convert_fusion
  (30 shorter events, 3.5 us)
Async XLA Ops:
  7.2 232.6 %copy-start = (bf16[1,7168,128]{2,1,0:T(8,128)(2,1)S(1)}, bf16[1,7168,128]{2,1,0:T(8,128)(2,1)}, u32[]{:S(2)}) copy-start(bf16[1,7168,128]{2,1,0:T(8,128)(2,1)} %param.11) | copy-start | bytes 5505028
  7.2 239.9 %all-gather.2.cloned.1.call-start = ((), (), s32[]{:S(2)}) async-start(), calls=%async_computation.5 | async-start | bytes 11698176 | tf_op jit(solution)/shard_map/all_gather | solution.py:43
  37.2 326.3 %reduce-scatter.2.cloned.1.call-start = ((), (), s32[]{:S(2)}) async-start(), calls=%async_computation.6 | async-start | bytes 11698176 | tf_op jit(solution)/shard_map/reduce_scatter | solution.py:66
  239.8 4.3 %copy-start.2 = (bf16[16,48,7168]{2,1,0:T(8,128)(2,1)}, bf16[16,48,7168]{2,1,0:T(8,128)(2,1)S(1)}, u32[]{:S(2)}) copy-start(bf16[16,48,7168]{2,1,0:T(8,128)(2,1)S(1)} %all_to_all.22) | copy-start | bytes 33030148
  239.8 4.3 %copy-start.3 = (bf16[1,7168,128]{2,1,0:T(8,128)(2,1)S(1)}, bf16[1,7168,128]{2,1,0:T(8,128)(2,1)}, u32[]{:S(2)}) copy-start(bf16[1,7168,128]{2,1,0:T(8,128)(2,1)} %param.12) | copy-start | bytes 5505028
  365.8 19.2 %all-to-all-start.3 = ((bf16[8,6,7168]{2,1,0:T(8,128)(2,1)}), bf16[8,6,7168]{2,1,0:T(8,128)(2,1)S(1)}, u32[]{:S(2)}, u32[]{:S(2)}) async-start(bf16[8,6,7168]{2,1,0:T(8,128)(2,1)} %reshape.76), calls=%async_computation.4 | async-start | bytes 1835008 | tf_op jit(solution)/shard_map/all_to_all | solution.py:78
  371.3 15.9 %copy-start.1 = (bf16[1,7168,128]{2,1,0:T(8,128)(2,1)S(1)}, bf16[1,7168,128]{2,1,0:T(8,128)(2,1)}, u32[]{:S(2)}) copy-start(bf16[1,7168,128]{2,1,0:T(8,128)(2,1)} %param.11) | copy-start | bytes 5505028
Sparse Core Ops, SparseCore 0:
  37.3 196.1 all-gather.1
  277.1 86.3 reduce-scatter.1
